TPU v7x, 32 devices: a whole 2x2x4 slice. The times are simulated.
32 devices in a mesh: seq: 8 (over z, x), head: 4 (over y, core), batch: 1.
Axes of the slice: x: 2, y: 2, z: 4, core: 2. Of those that a mesh axis runs over, the one named last changes fastest.
Arguments:
- queries: bfloat16 [2048, 4096], P(('batch', 'seq', 'head')), may hold values from -6 to 6
- keys: bfloat16 [2048, 512], P(('batch', 'seq', 'head')), may hold values from -6 to 6
- values: bfloat16 [2048, 512], P(('batch', 'seq', 'head')), may hold values from -6 to 6
- page_of_block: int32 [4], P('batch'), may hold values from 0 to 2, never falling along the last dimension, each value on 1 to 2 neighbouring positions
- links: int32 [4, 4], P('batch'), may hold values 0 or 1
Outputs:
- attended: bfloat16 [2048, 4096], P(('batch', 'seq', 'head'))
Inputs may be any that keep to these rules, and one draw needn't show every extreme that they name: `page_of_block`: page numbers never fall from one block to the next.
All inputs are finite; a program needn't handle non-finite values.
Results may differ from a plain program's by a relative error of at most 0.0065.
Values may be sent and summed in bfloat16 or wider, within the bound.
No kernel may reach another device: no remote copies, remote signals or barrier semaphores. Data moves between devices by JAX's collectives and lax.ppermute only.
A program may use at most 64 MiB of HBM per device.

v0:
```python
import jax
import jax.numpy as jnp
from jax import lax
from jax.sharding import PartitionSpec as P

HEAD_SIZE = 128
BLK = 512


def local(queries, keys, values, page_of_block, links):
    query_all, key_local, value_local = (
        lax.all_to_all(queries, "head", split_axis=1, concat_axis=0, tiled=True),
        lax.all_to_all(keys, "head", split_axis=1, concat_axis=0, tiled=True),
        lax.all_to_all(values, "head", split_axis=1, concat_axis=0, tiled=True),
    )
    row_count = query_all.shape[0]
    kv_here = key_local.shape[1] // HEAD_SIZE
    group_width = query_all.shape[1] // HEAD_SIZE // kv_here
    first_row = lax.axis_index("seq") * row_count
    block_count = page_of_block.shape[0]
    block_ids = jnp.arange(block_count, dtype=jnp.int32)
    page_table = page_of_block.astype(jnp.float32)
    link_table = links.astype(jnp.float32)
    query_pos = first_row + jnp.arange(row_count, dtype=jnp.int32)
    query_onehot = (query_pos[:, None] // BLK == block_ids[None, :]).astype(jnp.float32)
    query_page = jnp.dot(query_onehot, page_table, precision=lax.Precision.HIGHEST)
    query_links = jnp.dot(query_onehot, link_table, precision=lax.Precision.HIGHEST)
    query_heads = query_all.reshape(row_count, kv_here, group_width, HEAD_SIZE)
    score_scale = HEAD_SIZE ** (-0.5)

    def block_step(running, key_block, value_block, offset):
        block_rows = key_block.shape[0]
        key_pos = offset + jnp.arange(block_rows, dtype=jnp.int32)
        key_onehot = (key_pos[:, None] // BLK == block_ids[None, :]).astype(jnp.float32)
        key_page = jnp.dot(key_onehot, page_table, precision=lax.Precision.HIGHEST)
        linked = jnp.dot(query_links, key_onehot.T, precision=lax.Precision.HIGHEST) > 0.5
        same_page = query_page[:, None] == key_page[None, :]
        allowed = jnp.where(same_page, key_pos[None, :] <= query_pos[:, None], linked)

        def attend(previous):
            maxima, totals, weighted = previous
            scores = (
                jnp.einsum(
                    "rkgd,pkd->kgrp",
                    query_heads,
                    key_block.reshape(block_rows, kv_here, HEAD_SIZE),
                    preferred_element_type=jnp.float32,
                )
                * score_scale
            )
            scores = jnp.where(allowed[None, None], scores, -1e30)
            new_max = jnp.maximum(maxima, jnp.max(scores, axis=-1))
            weights = jnp.where(allowed[None, None], jnp.exp(scores - new_max[..., None]), 0.0)
            factor = jnp.exp(maxima - new_max)
            totals = totals * factor + jnp.sum(weights, axis=-1)
            rounded = weights.astype(jnp.bfloat16)
            weighted = weighted * factor[..., None] + jnp.einsum(
                "kgrp,pkd->kgrd",
                rounded,
                value_block.reshape(block_rows, kv_here, HEAD_SIZE),
                preferred_element_type=jnp.float32,
            )
            return (new_max, totals, weighted)

        return lax.cond(jnp.any(allowed), attend, lambda previous: previous, running)

    initial = (
        jnp.full((kv_here, group_width, row_count), -1e30, jnp.float32),
        jnp.zeros((kv_here, group_width, row_count), jnp.float32),
        jnp.zeros((kv_here, group_width, row_count, HEAD_SIZE), jnp.float32),
    )
    running = initial
    key_piece = lax.all_gather(key_local, "seq", axis=0, tiled=True)
    value_piece = lax.all_gather(value_local, "seq", axis=0, tiled=True)
    piece_rows = key_piece.shape[0]
    sub_count = piece_rows // BLK
    key_split = key_piece.reshape(sub_count, BLK, key_piece.shape[1])
    value_split = value_piece.reshape(sub_count, BLK, value_piece.shape[1])

    def scan_step(state_now, scan_item):
        key_block, value_block, block_index = scan_item
        return (block_step(state_now, key_block, value_block, block_index * BLK), None)

    running, unused = lax.scan(
        scan_step, running, (key_split, value_split, jnp.arange(sub_count, dtype=jnp.int32))
    )
    maxima, totals, weighted = running
    outcome = weighted / totals[..., None]
    outcome = (
        outcome.transpose(2, 0, 1, 3)
        .reshape(row_count, kv_here * group_width * HEAD_SIZE)
        .astype(jnp.bfloat16)
    )
    return lax.all_to_all(outcome, "head", split_axis=0, concat_axis=1, tiled=True)


def solution(mesh):
    in_specs = (
        P(("batch", "seq", "head"), None),
        P(("batch", "seq", "head"), None),
        P(("batch", "seq", "head"), None),
        P("batch"),
        P("batch", None),
    )
    out_specs = P(("batch", "seq", "head"), None)
    return jax.shard_map(local, mesh=mesh, in_specs=in_specs, out_specs=out_specs, check_vma=False)
```

profile of v0, /device:TPU:0, one launch (start us, length us, event | category | flops | bytes accessed | tf_op | source)
XLA Modules:
  0.0 122.0 jit_solution(15843513809518971838)
XLA Ops:
  0.0 0.8 copy-done
  0.8 0.6 copy_bitcast_fusion.2
  1.5 4.3 %all-to-all-start = ((bf16[64,4,128]{2,0,1:T(8,128)(2,1)}), bf16[64,4,128]{2,0,1:T(8,128)(2,1)S(1)}, u32[]{:S(2)}, u32[]{:S(2)}) async-start(bf16[64,4,128]{2,0,1:T(8,128)(2,1)} %copy_bitcast_fusion.2), calls=%async_computation | async-start | bytes 131072 | tf_op jit(solution)/shard_map/all_to_all | solution.py:13
  5.8 1.5 %copy_bitcast_fusion.1 = bf16[64,4,128]{2,0,1:T(8,128)(2,1)} fusion(bf16[64,512]{1,0:T(8,128)(2,1)} %param.11), kind=kLoop, calls=%fused_computation.53 | loop fusion | bytes 131072 | tf_op jit(solution)/shard_map/all_to_all | solution.py:14
  7.2 0.9 fusion.41
  8.1 1.7 %all-to-all-done = bf16[64,4,128]{2,0,1:T(8,128)(2,1)S(1)} async-done(((bf16[64,4,128]{2,0,1:T(8,128)(2,1)}), bf16[64,4,128]{2,0,1:T(8,128)(2,1)S(1)}, u32[]{:S(2)}, u32[]{:S(2)}) %all-to-all-start) | async-done | bytes 65568 | tf_op jit(solution)/shard_map/all_to_all | solution.py:13
  9.9 3.3 %all-to-all-start.2 = ((bf16[64,4,128]{2,0,1:T(8,128)(2,1)}), bf16[64,4,128]{2,0,1:T(8,128)(2,1)S(1)}, u32[]{:S(2)}, u32[]{:S(2)}) async-start(bf16[64,4,128]{2,0,1:T(8,128)(2,1)} %copy_bitcast_fusion.1), calls=%async_computation.2 | async-start | bytes 131072 | tf_op jit(solution)/shard_map/all_to_all | solution.py:14
  13.2 0.8 fusion.42
  14.0 0.7 convert_element_type.31
  14.7 1.9 %copy.43 = bf16[8,4,8,1024]{3,2,0,1:T(8,128)(2,1)} copy(bf16[8,4,8,1024]{3,2,1,0:T(8,128)(2,1)} %bitcast.120) | data formatting | bytes 1048576 | tf_op jit(solution)/shard_map/all_to_all | solution.py:12
  16.6 0.6 all-to-all-done.2
  17.2 3.5 %all-to-all-start.1 = ((bf16[64,4,1024]{2,0,1:T(8,128)(2,1)}), bf16[64,4,1024]{2,0,1:T(8,128)(2,1)S(1)}, u32[]{:S(2)}, u32[]{:S(2)}) async-start(bf16[64,4,1024]{2,0,1:T(8,128)(2,1)} %bitcast.104), calls=%async_computation.1 | async-start | bytes 1048576 | tf_op jit(solution)/shard_map/all_to_all | solution.py:12
  20.7 32.4 %all_gather.6 = bf16[2048,128]{1,0:T(8,128)(2,1)S(1)} all-gather(bf16[256,128]{1,0:T(8,128)(2,1)S(1)} %bitcast.122), channel_id=1, replica_groups=mesh['seq'=8,'head'=4,'batch'=1] {'seq'}, dimensions={0}, use_global_device_ids=true | all-gather | bytes 589824 | tf_op jit(solution)/shard_map/all_gather | solution.py:73
  53.1 31.2 %all_gather.7 = bf16[2048,128]{1,0:T(8,128)(2,1)S(1)} all-gather(bf16[256,128]{1,0:T(8,128)(2,1)S(1)} %bitcast.123), channel_id=1, replica_groups=mesh['seq'=8,'head'=4,'batch'=1] {'seq'}, dimensions={0}, use_global_device_ids=true | all-gather | bytes 589824 | tf_op jit(solution)/shard_map/all_gather | solution.py:74
  84.3 0.0 all-to-all-done.1
  84.3 0.1 copy.39
  84.4 0.1 copy.31
  84.4 0.1 broadcast_in_dim.54
  84.5 23.9 %while.19 = (s32[]{:T(128)}, f32[1,8,256]{2,1,0:T(8,128)S(1)}, f32[1,8,256]{2,1,0:T(8,128)S(1)}, f32[1,8,256,128]{3,2,1,0:T(8,128)S(1)}, f32[256]{0:T(256)S(1)},...) while((s32[]{:T(128)}, f32[1,8,256]{2,1,0:T(8,128)S(1)}, ...), condition=%wide.region_6.7_spmd.clone.clone, body=%wide.region_0.6_spmd.clone.clone.sunk | while | flops 558016768 | bytes 16143707 | solution.py:84
  84.6 0.6 dynamic_slice.42
  85.8 0.3 fusion.60
  86.1 1.1 fusion.61
  87.9 3.5 %conditional.4 = ((f32[1,8,256]{2,1,0:T(8,128)S(1)}, f32[1,8,256]{2,1,0:T(8,128)S(1)}, f32[1,8,256,128]{3,2,1,0:T(8,128)S(1)})) conditional(s32[]{:T(128)} %convert_element_type.56, (f32[1,8,256]{2,1,0:T(8,128)S(1)}, f32[1,8,256]{2,1,0:T(8,128)S(1)}, f32[1,8,256,128]{3,2,1,0:T(8,128)S(1)}) %tuple.66, (pred[256,512]{0,1:T(8,128)(4,1)S(1)}, ...), branch_computations={%region_2.2_spmd, %region_3.5_spmd} | conditional | flops 551032832 | bytes 15990824 | solution.py:65
  87.9 0.8 fusion.2
  88.7 1.6 %fusion.12 = f32[1,8,256,128]{3,2,1,0:T(8,128)S(1)} fusion(f32[512,256,8]{1,0,2:T(8,128)S(1)} %get-tuple-element.409, f32[8,256]{1,0:T(8,128)S(1)} %bitcast.113, pred[256,512]{0,1:T(8,128)(4,1)S(1)} %get-tuple-element.245, f32[1,8,256,128]{3,2,1,0:T(8,128)S(1)} %get-tuple-element.250, f32[8,256]{1,0:T(8,128)S(1)} %get-tuple-element.406, ...), kind=kOutput, calls=%fused_computation.10 | convolution fusion | flops 274202624 | bytes 6569988 | tf_op jit(solution)/shard_map/while/body/eval_jaxpr/cond/branch_1_fun/kgrp,pkd->kgrd/dot_general | solution.py:57
  90.4 1.0 fusion.4
  91.4 0.6 dynamic_slice.42
  92.7 0.3 fusion.60
  93.0 1.1 fusion.61
  94.8 3.5 %conditional.4 = ((f32[1,8,256]{2,1,0:T(8,128)S(1)}, f32[1,8,256]{2,1,0:T(8,128)S(1)}, f32[1,8,256,128]{3,2,1,0:T(8,128)S(1)})) conditional(s32[]{:T(128)} %convert_element_type.56, (f32[1,8,256]{2,1,0:T(8,128)S(1)}, f32[1,8,256]{2,1,0:T(8,128)S(1)}, f32[1,8,256,128]{3,2,1,0:T(8,128)S(1)}) %tuple.66, (pred[256,512]{0,1:T(8,128)(4,1)S(1)}, ...), branch_computations={%region_2.2_spmd, %region_3.5_spmd} | conditional | flops 551032832 | bytes 15990824 | solution.py:65
  94.8 0.8 fusion.2
  95.6 1.6 %fusion.12 = f32[1,8,256,128]{3,2,1,0:T(8,128)S(1)} fusion(f32[512,256,8]{1,0,2:T(8,128)S(1)} %get-tuple-element.409, f32[8,256]{1,0:T(8,128)S(1)} %bitcast.113, pred[256,512]{0,1:T(8,128)(4,1)S(1)} %get-tuple-element.245, f32[1,8,256,128]{3,2,1,0:T(8,128)S(1)} %get-tuple-element.250, f32[8,256]{1,0:T(8,128)S(1)} %get-tuple-element.406, ...), kind=kOutput, calls=%fused_computation.10 | convolution fusion | flops 274202624 | bytes 6569988 | tf_op jit(solution)/shard_map/while/body/eval_jaxpr/cond/branch_1_fun/kgrp,pkd->kgrd/dot_general | solution.py:57
  97.2 1.0 fusion.4
  98.3 0.6 dynamic_slice.42
  99.5 0.3 fusion.60
  99.8 1.1 fusion.61
  101.7 0.6 dynamic_slice.42
  102.9 0.3 fusion.60
  103.2 1.1 fusion.61
  105.0 3.5 %conditional.4 = ((f32[1,8,256]{2,1,0:T(8,128)S(1)}, f32[1,8,256]{2,1,0:T(8,128)S(1)}, f32[1,8,256,128]{3,2,1,0:T(8,128)S(1)})) conditional(s32[]{:T(128)} %convert_element_type.56, (f32[1,8,256]{2,1,0:T(8,128)S(1)}, f32[1,8,256]{2,1,0:T(8,128)S(1)}, f32[1,8,256,128]{3,2,1,0:T(8,128)S(1)}) %tuple.66, (pred[256,512]{0,1:T(8,128)(4,1)S(1)}, ...), branch_computations={%region_2.2_spmd, %region_3.5_spmd} | conditional | flops 551032832 | bytes 15990824 | solution.py:65
  105.0 0.8 fusion.2
  105.8 1.6 %fusion.12 = f32[1,8,256,128]{3,2,1,0:T(8,128)S(1)} fusion(f32[512,256,8]{1,0,2:T(8,128)S(1)} %get-tuple-element.409, f32[8,256]{1,0:T(8,128)S(1)} %bitcast.113, pred[256,512]{0,1:T(8,128)(4,1)S(1)} %get-tuple-element.245, f32[1,8,256,128]{3,2,1,0:T(8,128)S(1)} %get-tuple-element.250, f32[8,256]{1,0:T(8,128)S(1)} %get-tuple-element.406, ...), kind=kOutput, calls=%fused_computation.10 | convolution fusion | flops 274202624 | bytes 6569988 | tf_op jit(solution)/shard_map/while/body/eval_jaxpr/cond/branch_1_fun/kgrp,pkd->kgrd/dot_general | solution.py:57
  107.4 1.0 fusion.4
  108.5 0.3 fusion.40
  108.9 0.3 copy.32
  109.2 0.2 convert_element_type.35
  109.4 11.7 %all_to_all.70 = bf16[4,64,1024]{2,1,0:T(8,128)(2,1)S(1)} all-to-all(bf16[4,64,1024]{2,1,0:T(8,128)(2,1)S(1)} %convert_element_type.35), channel_id=1, replica_groups=mesh['seq'=8,'head'=4,'batch'=1] {'head'}, dimensions={0} | all-to-all | bytes 1048576 | tf_op jit(solution)/shard_map/all_to_all | solution.py:94
  121.2 0.8 copy.38
  (23 shorter events, 0.2 us)
Async XLA Ops:
  0.0 0.8 copy-start
  1.5 8.4 %all-to-all-start = ((bf16[64,4,128]{2,0,1:T(8,128)(2,1)}), bf16[64,4,128]{2,0,1:T(8,128)(2,1)S(1)}, u32[]{:S(2)}, u32[]{:S(2)}) async-start(bf16[64,4,128]{2,0,1:T(8,128)(2,1)} %copy_bitcast_fusion.2), calls=%async_computation | async-start | bytes 131072 | tf_op jit(solution)/shard_map/all_to_all | solution.py:13
  9.9 7.4 %all-to-all-start.2 = ((bf16[64,4,128]{2,0,1:T(8,128)(2,1)}), bf16[64,4,128]{2,0,1:T(8,128)(2,1)S(1)}, u32[]{:S(2)}, u32[]{:S(2)}) async-start(bf16[64,4,128]{2,0,1:T(8,128)(2,1)} %copy_bitcast_fusion.1), calls=%async_computation.2 | async-start | bytes 131072 | tf_op jit(solution)/shard_map/all_to_all | solution.py:14
  17.2 67.0 %all-to-all-start.1 = ((bf16[64,4,1024]{2,0,1:T(8,128)(2,1)}), bf16[64,4,1024]{2,0,1:T(8,128)(2,1)S(1)}, u32[]{:S(2)}, u32[]{:S(2)}) async-start(bf16[64,4,1024]{2,0,1:T(8,128)(2,1)} %bitcast.104), calls=%async_computation.1 | async-start | bytes 1048576 | tf_op jit(solution)/shard_map/all_to_all | solution.py:12
where the time goes:
time: 123 us; the launch traced here: 122 us
  blocking collectives  75.2 us (61%)
  matrix products  14.7 us (12%)
  starting transfers between devices  11 us (9%)
  local copies, waits for them, and re-layouts  8.84 us (7%)
  loops' own time  5.51 us (4%)
  other arithmetic  4.22 us (3%)
  waiting for transfers between devices  2.38 us (2%)
    all_gather x1, blocking collectives, local(): key_piece = lax.all_gather(key_local, 'seq', axis=0, tiled=True)  32.4 us
    all_gather x1, blocking collectives, local(): value_piece = lax.all_gather(value_local, 'seq', axis=0, tiled=True)  31.2 us
    all_to_all x1, blocking collectives, local(): lax.all_to_all(outcome, 'head', split_axis=0, concat_axis=1, tiled=True)  11.7 us
    another operation x1, loops' own time, local(): lax.scan(scan_step, running, (key_split, value_split, jnp.arange(sub_coun...  5.34 us
    dot_general x3, matrix products, attend(): jnp.einsum('kgrp,pkd->kgrd', rounded, value_block.reshape(block_rows, kv_...  4.83 us
    dot_general x4, matrix products, block_step(): jnp.dot(query_links, key_onehot.T, precision=lax.Precision.HIGHEST) > 0.5  4.53 us
    all_to_all x1, starting transfers between devices, local(): lax.all_to_all(keys, 'head', split_axis=1, concat_axis=0, tiled=True)  4.26 us
    all_to_all x1, starting transfers between devices, local(): lax.all_to_all(queries, 'head', split_axis=1, concat_axis=0, tiled=True)  3.47 us
  transfers between devices with their start and end apart: 3, of which 2 were waited for; matrix products, arithmetic and copies ran while one was open for 5% of the time, Pallas kernels for 0%

commit v1 on v0

--- a/solution.py
+++ b/solution.py
@@ -7,10 +7,33 @@
 BLK = 512
 
 
+def split_up(value, dim, size):
+    before, after = (value.shape[:dim], value.shape[dim + 1 :])
+    return jnp.moveaxis(value.reshape(*before, size, -1, *after), dim, 0)
+
+
+def joined_along(parts, dim):
+    parts = jnp.moveaxis(parts, 0, dim)
+    dims = parts.shape
+    return parts.reshape(*dims[:dim], dims[dim] * dims[dim + 1], *dims[dim + 2 :])
+
+
+def sent_to_each(shard, axis, split_dim, concat_dim):
+    devices, place = (lax.axis_size(axis), lax.axis_index(axis))
+    pieces = split_up(shard, split_dim, devices)
+    out = pieces
+    for step in range(1, devices):
+        target, source = ((place + step) % devices, (place - step) % devices)
+        sent = lax.dynamic_index_in_dim(pieces, target, 0)
+        other = lax.ppermute(sent, axis, [(i, (i + step) % devices) for i in range(devices)])
+        out = lax.dynamic_update_slice_in_dim(out, other, source, axis=0)
+    return joined_along(out, concat_dim)
+
+
 def local(queries, keys, values, page_of_block, links):
     query_all, key_local, value_local = (
         lax.all_to_all(queries, "head", split_axis=1, concat_axis=0, tiled=True),
-        lax.all_to_all(keys, "head", split_axis=1, concat_axis=0, tiled=True),
+        sent_to_each(keys, "head", 1, 0),
         lax.all_to_all(values, "head", split_axis=1, concat_axis=0, tiled=True),
     )
     row_count = query_all.shape[0]

time: 123 us -> 119 us (0.967)
  waiting for transfers between devices: 2.38 us -> 0.01 us
    ppermute x0 -> x3, starting transfers between devices: none -> 4.51 us  [sent_to_each(): lax.ppermute(sent, axis, [(i, (i + step) % devices) for i in range(device...]
    all_to_all x1 -> x0, starting transfers between devices: 4.26 us -> none  [local(): lax.all_to_all(keys, 'head', split_axis=1, concat_axis=0, tiled=True)]
    all_to_all x1 -> x0, waiting for transfers between devices: 1.74 us -> none  [local(): lax.all_to_all(keys, 'head', split_axis=1, concat_axis=0, tiled=True)]
  transfers between devices with their start and end apart: 3 -> 5, of which waited for: 2 -> 0; matrix products, arithmetic and copies ran while one was open for 5% -> 5% of each run, Pallas kernels for 0% -> 0%
where the time goes in v1:
time: 119 us
  blocking collectives  74.8 us (63%)
  matrix products  14.7 us (12%)
  starting transfers between devices  11.3 us (9%)
  local copies, waits for them, and re-layouts  8 us (7%)
  loops' own time  5.51 us (5%)
  other arithmetic  4.22 us (4%)
    all_gather x1, blocking collectives, local(): key_piece = lax.all_gather(key_local, 'seq', axis=0, tiled=True)  31.9 us
    all_gather x1, blocking collectives, local(): value_piece = lax.all_gather(value_local, 'seq', axis=0, tiled=True)  31.2 us
    all_to_all x1, blocking collectives, local(): lax.all_to_all(outcome, 'head', split_axis=0, concat_axis=1, tiled=True)  11.7 us
    another operation x1, loops' own time, local(): lax.scan(scan_step, running, (key_split, value_split, jnp.arange(sub_coun...  5.34 us
    dot_general x3, matrix products, attend(): jnp.einsum('kgrp,pkd->kgrd', rounded, value_block.reshape(block_rows, kv_...  4.83 us
    dot_general x4, matrix products, block_step(): jnp.dot(query_links, key_onehot.T, precision=lax.Precision.HIGHEST) > 0.5  4.53 us
    ppermute x3, starting transfers between devices, sent_to_each(): lax.ppermute(sent, axis, [(i, (i + step) % devices) for i in range(device...  4.51 us
    all_to_all x1, starting transfers between devices, local(): lax.all_to_all(queries, 'head', split_axis=1, concat_axis=0, tiled=True)  3.48 us
  transfers between devices with their start and end apart: 5, of which 0 were waited for; matrix products, arithmetic and copies ran while one was open for 5% of the time, Pallas kernels for 0%

profile of v1, /device:TPU:0, one launch (start us, length us, event | category | flops | bytes accessed | tf_op | source)
XLA Modules:
  0.0 118.7 jit_solution(9296855060029935273)
XLA Ops:
  0.0 0.9 reshape.161
  0.9 0.1 dynamic-slice_bitcast_fusion
  1.0 0.5 collective-permute-start
  1.6 2.6 %collective-permute-start.1 = (bf16[1,64,128]{2,0,1:T(2,128)(2,1)S(1)}, bf16[1,64,128]{2,0,1:T(2,128)(2,1)S(1)}, u32[]{:S(2)}, u32[]{:S(2)}) collective-permute-start(bf16[1,64,128]{2,0,1:T(2,128)(2,1)S(1)} %get-tuple-element.415), channel_id=1, source_target_pairs={{0,2},{1,3},{2,0},{3,1},{4,6},{5,7},{6,4},{7,5},{8,10},{9,11},{10,... | collective-permute-start | bytes 49160 | tf_op jit(solution)/shard_map/ppermute | solution.py:28
  4.2 1.4 %collective-permute-start.2 = (bf16[1,64,128]{2,0,1:T(2,128)(2,1)S(1)}, bf16[1,64,128]{2,0,1:T(2,128)(2,1)S(1)}, u32[]{:S(2)}, u32[]{:S(2)}) collective-permute-start(bf16[1,64,128]{2,0,1:T(2,128)(2,1)S(1)} %get-tuple-element.414), channel_id=1, source_target_pairs={{0,3},{1,0},{2,1},{3,2},{4,7},{5,4},{6,5},{7,6},{8,11},{9,8},{10,9... | collective-permute-start | bytes 49160 | tf_op jit(solution)/shard_map/ppermute | solution.py:28
  5.5 0.6 copy_bitcast_fusion.1
  6.2 3.3 %all-to-all-start.1 = ((bf16[64,4,128]{2,0,1:T(8,128)(2,1)}), bf16[64,4,128]{2,0,1:T(8,128)(2,1)S(1)}, u32[]{:S(2)}, u32[]{:S(2)}) async-start(bf16[64,4,128]{2,0,1:T(8,128)(2,1)} %copy_bitcast_fusion.1), calls=%async_computation.1 | async-start | bytes 131072 | tf_op jit(solution)/shard_map/all_to_all | solution.py:37
  9.5 0.9 fusion.41
  10.4 0.9 fusion.42
  11.3 0.7 convert_element_type.31
  12.0 1.9 %copy.42 = bf16[8,4,8,1024]{3,2,0,1:T(8,128)(2,1)} copy(bf16[8,4,8,1024]{3,2,1,0:T(8,128)(2,1)} %bitcast.121) | data formatting | bytes 1048576 | tf_op jit(solution)/shard_map/all_to_all | solution.py:35
  13.9 0.1 dynamic_update_slice.9
  14.1 0.2 dynamic_update_slice.10
  14.2 0.2 dynamic_update_slice.11
  14.4 3.5 %all-to-all-start = ((bf16[64,4,1024]{2,0,1:T(8,128)(2,1)}), bf16[64,4,1024]{2,0,1:T(8,128)(2,1)S(1)}, u32[]{:S(2)}, u32[]{:S(2)}) async-start(bf16[64,4,1024]{2,0,1:T(8,128)(2,1)} %bitcast.104), calls=%async_computation | async-start | bytes 1048576 | tf_op jit(solution)/shard_map/all_to_all | solution.py:35
  17.9 31.9 %all_gather.6 = bf16[2048,128]{1,0:T(8,128)(2,1)S(1)} all-gather(bf16[256,128]{1,0:T(8,128)(2,1)S(1)} %bitcast.124), channel_id=1, replica_groups=mesh['seq'=8,'head'=4,'batch'=1] {'seq'}, dimensions={0}, use_global_device_ids=true | all-gather | bytes 589824 | tf_op jit(solution)/shard_map/all_gather | solution.py:96
  49.8 31.2 %all_gather.7 = bf16[2048,128]{1,0:T(8,128)(2,1)S(1)} all-gather(bf16[256,128]{1,0:T(8,128)(2,1)S(1)} %bitcast.123), channel_id=1, replica_groups=mesh['seq'=8,'head'=4,'batch'=1] {'seq'}, dimensions={0}, use_global_device_ids=true | all-gather | bytes 589824 | tf_op jit(solution)/shard_map/all_gather | solution.py:97
  81.0 0.1 copy.39
  81.3 24.0 %while.19 = (s32[]{:T(128)}, f32[1,8,256]{2,1,0:T(8,128)S(1)}, f32[1,8,256]{2,1,0:T(8,128)S(1)}, f32[1,8,256,128]{3,2,1,0:T(8,128)S(1)}, f32[256]{0:T(256)S(1)},...) while((s32[]{:T(128)}, f32[1,8,256]{2,1,0:T(8,128)S(1)}, ...), condition=%wide.region_6.7_spmd.clone.clone, body=%wide.region_0.6_spmd.clone.clone.sunk | while | flops 558016768 | bytes 16143707 | solution.py:107
  81.3 0.6 dynamic_slice.55
  82.5 0.3 fusion.59
  82.8 1.1 fusion.60
  84.6 3.5 %conditional.4 = ((f32[1,8,256]{2,1,0:T(8,128)S(1)}, f32[1,8,256]{2,1,0:T(8,128)S(1)}, f32[1,8,256,128]{3,2,1,0:T(8,128)S(1)})) conditional(s32[]{:T(128)} %convert_element_type.56, (f32[1,8,256]{2,1,0:T(8,128)S(1)}, f32[1,8,256]{2,1,0:T(8,128)S(1)}, f32[1,8,256,128]{3,2,1,0:T(8,128)S(1)}) %tuple.68, (pred[256,512]{0,1:T(8,128)(4,1)S(1)}, ...), branch_computations={%region_2.2_spmd, %region_3.5_spmd} | conditional | flops 551032832 | bytes 15990824 | solution.py:88
  84.6 0.8 fusion.2
  85.4 1.6 %fusion.12 = f32[1,8,256,128]{3,2,1,0:T(8,128)S(1)} fusion(f32[512,256,8]{1,0,2:T(8,128)S(1)} %get-tuple-element.409, f32[8,256]{1,0:T(8,128)S(1)} %bitcast.113, pred[256,512]{0,1:T(8,128)(4,1)S(1)} %get-tuple-element.245, f32[1,8,256,128]{3,2,1,0:T(8,128)S(1)} %get-tuple-element.250, f32[8,256]{1,0:T(8,128)S(1)} %get-tuple-element.406, ...), kind=kOutput, calls=%fused_computation.10 | convolution fusion | flops 274202624 | bytes 6569988 | tf_op jit(solution)/shard_map/while/body/eval_jaxpr/cond/branch_1_fun/kgrp,pkd->kgrd/dot_general | solution.py:80
  87.1 1.0 fusion.4
  88.1 0.6 dynamic_slice.55
  89.4 0.3 fusion.59
  89.7 1.1 fusion.60
  91.5 3.5 %conditional.4 = ((f32[1,8,256]{2,1,0:T(8,128)S(1)}, f32[1,8,256]{2,1,0:T(8,128)S(1)}, f32[1,8,256,128]{3,2,1,0:T(8,128)S(1)})) conditional(s32[]{:T(128)} %convert_element_type.56, (f32[1,8,256]{2,1,0:T(8,128)S(1)}, f32[1,8,256]{2,1,0:T(8,128)S(1)}, f32[1,8,256,128]{3,2,1,0:T(8,128)S(1)}) %tuple.68, (pred[256,512]{0,1:T(8,128)(4,1)S(1)}, ...), branch_computations={%region_2.2_spmd, %region_3.5_spmd} | conditional | flops 551032832 | bytes 15990824 | solution.py:88
  91.5 0.8 fusion.2
  92.3 1.6 %fusion.12 = f32[1,8,256,128]{3,2,1,0:T(8,128)S(1)} fusion(f32[512,256,8]{1,0,2:T(8,128)S(1)} %get-tuple-element.409, f32[8,256]{1,0:T(8,128)S(1)} %bitcast.113, pred[256,512]{0,1:T(8,128)(4,1)S(1)} %get-tuple-element.245, f32[1,8,256,128]{3,2,1,0:T(8,128)S(1)} %get-tuple-element.250, f32[8,256]{1,0:T(8,128)S(1)} %get-tuple-element.406, ...), kind=kOutput, calls=%fused_computation.10 | convolution fusion | flops 274202624 | bytes 6569988 | tf_op jit(solution)/shard_map/while/body/eval_jaxpr/cond/branch_1_fun/kgrp,pkd->kgrd/dot_general | solution.py:80
  93.9 1.0 fusion.4
  95.0 0.6 dynamic_slice.55
  96.2 0.3 fusion.59
  96.5 1.1 fusion.60
  98.4 0.6 dynamic_slice.55
  99.6 0.3 fusion.59
  99.9 1.1 fusion.60
  101.7 3.5 %conditional.4 = ((f32[1,8,256]{2,1,0:T(8,128)S(1)}, f32[1,8,256]{2,1,0:T(8,128)S(1)}, f32[1,8,256,128]{3,2,1,0:T(8,128)S(1)})) conditional(s32[]{:T(128)} %convert_element_type.56, (f32[1,8,256]{2,1,0:T(8,128)S(1)}, f32[1,8,256]{2,1,0:T(8,128)S(1)}, f32[1,8,256,128]{3,2,1,0:T(8,128)S(1)}) %tuple.68, (pred[256,512]{0,1:T(8,128)(4,1)S(1)}, ...), branch_computations={%region_2.2_spmd, %region_3.5_spmd} | conditional | flops 551032832 | bytes 15990824 | solution.py:88
  101.7 0.8 fusion.2
  102.5 1.6 %fusion.12 = f32[1,8,256,128]{3,2,1,0:T(8,128)S(1)} fusion(f32[512,256,8]{1,0,2:T(8,128)S(1)} %get-tuple-element.409, f32[8,256]{1,0:T(8,128)S(1)} %bitcast.113, pred[256,512]{0,1:T(8,128)(4,1)S(1)} %get-tuple-element.245, f32[1,8,256,128]{3,2,1,0:T(8,128)S(1)} %get-tuple-element.250, f32[8,256]{1,0:T(8,128)S(1)} %get-tuple-element.406, ...), kind=kOutput, calls=%fused_computation.10 | convolution fusion | flops 274202624 | bytes 6569988 | tf_op jit(solution)/shard_map/while/body/eval_jaxpr/cond/branch_1_fun/kgrp,pkd->kgrd/dot_general | solution.py:80
  104.2 1.0 fusion.4
  105.2 0.3 fusion.40
  105.6 0.3 copy.33
  105.9 0.2 convert_element_type.35
  106.2 11.7 %all_to_all.51 = bf16[4,64,1024]{2,1,0:T(8,128)(2,1)S(1)} all-to-all(bf16[4,64,1024]{2,1,0:T(8,128)(2,1)S(1)} %convert_element_type.35), channel_id=1, replica_groups=mesh['seq'=8,'head'=4,'batch'=1] {'head'}, dimensions={0} | all-to-all | bytes 1048576 | tf_op jit(solution)/shard_map/all_to_all | solution.py:117
  117.9 0.8 copy.38
  (32 shorter events, 0.3 us)
Async XLA Ops:
  0.0 5.5 %copy-start = (bf16[64,512]{1,0:T(8,128)(2,1)S(1)}, bf16[64,512]{1,0:T(8,128)(2,1)}, u32[]{:S(2)}) copy-start(bf16[64,512]{1,0:T(8,128)(2,1)} %param.11) | copy-start | bytes 196612
  1.0 12.9 %collective-permute-start = (bf16[1,64,128]{2,0,1:T(2,128)(2,1)S(1)}, bf16[1,64,128]{2,0,1:T(2,128)(2,1)S(1)}, u32[]{:S(2)}, u32[]{:S(2)}) collective-permute-start(bf16[1,64,128]{2,0,1:T(2,128)(2,1)S(1)} %get-tuple-element.416), channel_id=1, source_target_pairs={{0,1},{1,2},{2,3},{3,0},{4,5},{5,6},{6,7},{7,4},{8,9},{9,10},{10,1... | collective-permute-start | bytes 49160 | tf_op jit(solution)/shard_map/ppermute | solution.py:28
  1.6 12.5 %collective-permute-start.1 = (bf16[1,64,128]{2,0,1:T(2,128)(2,1)S(1)}, bf16[1,64,128]{2,0,1:T(2,128)(2,1)S(1)}, u32[]{:S(2)}, u32[]{:S(2)}) collective-permute-start(bf16[1,64,128]{2,0,1:T(2,128)(2,1)S(1)} %get-tuple-element.415), channel_id=1, source_target_pairs={{0,2},{1,3},{2,0},{3,1},{4,6},{5,7},{6,4},{7,5},{8,10},{9,11},{10,... | collective-permute-start | bytes 49160 | tf_op jit(solution)/shard_map/ppermute | solution.py:28
  4.2 10.1 %collective-permute-start.2 = (bf16[1,64,128]{2,0,1:T(2,128)(2,1)S(1)}, bf16[1,64,128]{2,0,1:T(2,128)(2,1)S(1)}, u32[]{:S(2)}, u32[]{:S(2)}) collective-permute-start(bf16[1,64,128]{2,0,1:T(2,128)(2,1)S(1)} %get-tuple-element.414), channel_id=1, source_target_pairs={{0,3},{1,0},{2,1},{3,2},{4,7},{5,4},{6,5},{7,6},{8,11},{9,8},{10,9... | collective-permute-start | bytes 49160 | tf_op jit(solution)/shard_map/ppermute | solution.py:28
  6.2 8.2 %all-to-all-start.1 = ((bf16[64,4,128]{2,0,1:T(8,128)(2,1)}), bf16[64,4,128]{2,0,1:T(8,128)(2,1)S(1)}, u32[]{:S(2)}, u32[]{:S(2)}) async-start(bf16[64,4,128]{2,0,1:T(8,128)(2,1)} %copy_bitcast_fusion.1), calls=%async_computation.1 | async-start | bytes 131072 | tf_op jit(solution)/shard_map/all_to_all | solution.py:37
  14.4 66.6 %all-to-all-start = ((bf16[64,4,1024]{2,0,1:T(8,128)(2,1)}), bf16[64,4,1024]{2,0,1:T(8,128)(2,1)S(1)}, u32[]{:S(2)}, u32[]{:S(2)}) async-start(bf16[64,4,1024]{2,0,1:T(8,128)(2,1)} %bitcast.104), calls=%async_computation | async-start | bytes 1048576 | tf_op jit(solution)/shard_map/all_to_all | solution.py:35
